TPU v7x, 32 devices: a whole 2x2x4 slice. The times are simulated.
32 devices in a mesh: gx: 8 (over z, x), gy: 4 (over y, core).
Axes of the slice: x: 2, y: 2, z: 4, core: 2. Of those that a mesh axis runs over, the one named last changes fastest.
Arguments:
- control: float32 [75, 128, 1024], P(None, 'gy', 'gx'), may hold values from -6 to 6
- east_coeff: float32 [75, 128, 1024], P(None, 'gy', 'gx'), may hold values from 0.12 to 0.245
- north_coeff: float32 [75, 128, 1024], P(None, 'gy', 'gx'), may hold values from 0.12 to 0.245
- ocean_mask: int32 [75, 128, 1024], P(None, 'gy', 'gx'), may hold values 0 or 1
- corner_cells: int32 [4, 131072], P(None, ('gx', 'gy')), may hold values from 0 to 4095, as said below
- corner_weights: float32 [4, 131072], P(None, ('gx', 'gy')), may hold values from 0 to 1, as said below
- obs_value: float32 [75, 131072], P(None, ('gx', 'gy')), may hold values from -6 to 6
- obs_precision: float32 [75, 131072], P(None, ('gx', 'gy')), may hold values from 0.3 to 3
- slot_counts: int32 [32, 32], P(('gx', 'gy')), may hold values from 1 to 128, as said below
Outputs:
- gradient: float32 [75, 128, 1024], P(None, 'gy', 'gx')
- departures: float32 [75, 131072], P(None, ('gx', 'gy'))
Inputs may be any that keep to these rules, and one draw needn't show every extreme that they name: For each slot, corner_cells lists the cells (r, s), (r, s + 1), (r + 1, s), (r + 1, s + 1) of one grid cell with r < 31 and s < 127, numbered r * 128 + s in the holding device's tile, in that order. `corner_weights`: the four weights of a slot are the bilinear weights (1 - a)(1 - b), a(1 - b), (1 - a)b, ab of two fractions a, b in [0, 1]; they sum to 1. slot_counts[d, p] counts the live slots that device p holds for owner d; for every owner some device sends exactly 128 live slots.
All inputs are finite; a program needn't handle non-finite values. No bound on the sum of `ocean_mask` on one device may be relied on, other than what follows from the above.
Results may differ from a plain program's by a relative error of at most 0.00002.
Values sent between devices are 32-bit elements; how exact they have to be, the bound alone decides.
No kernel may reach another device: no remote copies, remote signals or barrier semaphores. Data moves between devices by JAX's collectives and lax.ppermute only.
A program may use at most 128 MiB of HBM per device.

v0:
```python
import jax
import jax.numpy as jnp
from jax import lax
from jax.sharding import PartitionSpec as P

STEPS = 4


def with_halo(x, sides, width):
    for axis, dim in sides:
        size, length = (lax.axis_size(axis), x.shape[dim])
        up = [(i, (i + 1) % size) for i in range(size)]
        down = [(j, i) for i, j in up]
        last = lax.slice_in_dim(x, length - width, length, axis=dim)
        first = lax.slice_in_dim(x, 0, width, axis=dim)
        before = lax.ppermute(last, axis, up)
        after = lax.ppermute(first, axis, down)
        x = jnp.concatenate([before, x, after], axis=dim)
    return x


def sweep(padded, east, north):
    centre = padded[:, 1:-1, 1:-1]
    return (
        centre
        + east[:, 1:-1, 1:-1] * (padded[:, 1:-1, 2:] - centre)
        - east[:, 1:-1, :-2] * (centre - padded[:, 1:-1, :-2])
        + north[:, 1:-1, 1:-1] * (padded[:, 2:, 1:-1] - centre)
        - north[:, :-2, 1:-1] * (centre - padded[:, :-2, 1:-1])
    )


def body(
    control,
    east_coeff,
    north_coeff,
    ocean_mask,
    corner_cells,
    corner_weights,
    obs_value,
    obs_precision,
    slot_counts,
):
    levels, tile_rows, tile_cols = control.shape
    lat_index = lax.axis_index("gy")
    total_rows = tile_rows * lax.axis_size("gy")
    masked = ocean_mask.astype(jnp.float32)
    stacked = jnp.stack([masked, east_coeff, north_coeff])
    margin = STEPS
    rimmed = with_halo(stacked, (("gx", 3), ("gy", 2)), STEPS)
    mask_wide = rimmed[0]
    east = rimmed[1][:, :, :-1] * mask_wide[:, :, :-1] * mask_wide[:, :, 1:]
    east = jnp.pad(east, ((0, 0), (0, 0), (0, 1)))
    north = rimmed[2][:, :-1, :] * mask_wide[:, :-1, :] * mask_wide[:, 1:, :]
    global_rows = lat_index * tile_rows - margin + jnp.arange(tile_rows + 2 * margin - 1)
    row_keep = ((global_rows >= 0) & (global_rows < total_rows - 1)).astype(jnp.float32)
    north = jnp.pad(north * row_keep[None, :, None], ((0, 0), (0, 1), (0, 0)))

    def diffuse(current):
        padded = with_halo(current, (("gx", 2), ("gy", 1)), STEPS)
        for sweep_count in range(STEPS):
            remain = STEPS - sweep_count
            height = tile_rows + 2 * remain
            width_now = tile_cols + 2 * remain
            padded = sweep(
                padded,
                east[:, sweep_count : sweep_count + height, sweep_count : sweep_count + width_now],
                north[:, sweep_count : sweep_count + height, sweep_count : sweep_count + width_now],
            )
        return padded

    background = diffuse(masked * control)
    flat = background.reshape(levels, -1)
    corners = corner_cells.shape[0]
    cell_list = corner_cells.reshape(-1)
    picked = jnp.take(flat, cell_list, axis=1).reshape(levels, corners, -1)
    equivalent = jnp.sum(picked * corner_weights[None, :, :], axis=1)
    slots = equivalent.shape[1]
    peers = lax.axis_size(("gx", "gy"))
    capacity = slots // peers
    received = lax.all_to_all(equivalent, ("gx", "gy"), split_axis=1, concat_axis=1, tiled=True)
    live = (slot_counts[0][:, None] > jnp.arange(capacity)[None, :]).reshape(slots)
    departures = jnp.where(live[None, :], obs_precision * (received - obs_value), jnp.float32(0.0))
    returned = lax.all_to_all(departures, ("gx", "gy"), split_axis=1, concat_axis=1, tiled=True)
    spread = (corner_weights[None, :, :] * returned[:, None, :]).reshape(levels, -1)
    adjoint = jnp.zeros((levels, tile_rows * tile_cols), jnp.float32).at[:, cell_list].add(spread)
    gradient = masked * (control + diffuse(adjoint.reshape(levels, tile_rows, tile_cols)))
    return (gradient, departures)


def solution(mesh):
    return jax.shard_map(
        body,
        mesh=mesh,
        in_specs=(
            P(None, "gy", "gx"),
            P(None, "gy", "gx"),
            P(None, "gy", "gx"),
            P(None, "gy", "gx"),
            P(None, ("gx", "gy")),
            P(None, ("gx", "gy")),
            P(None, ("gx", "gy")),
            P(None, ("gx", "gy")),
            P(("gx", "gy"), None),
        ),
        out_specs=(P(None, "gy", "gx"), P(None, ("gx", "gy"))),
        check_vma=False,
    )
```

profile of v0, /device:TPU:1, one launch (start us, length us, event | category | flops | bytes accessed | tf_op | source)
XLA Modules:
  0.0 347.6 jit_solution(17975862376519627742)
XLA Ops:
  0.6 2.4 copy.75
  3.0 1.6 convert_bitcast_fusion
  4.7 0.5 copy-done.15
  5.2 2.2 copy.81
  7.4 3.1 copy.82
  10.5 1.9 pad_maximum_fusion.13
  12.4 2.0 collective-permute-start.4
  14.4 3.0 collective-permute-start.5
  17.4 2.1 copy.103
  19.6 2.2 convert_multiply_fusion
  21.9 4.1 %collective-permute-start.1 = (f32[75,32,4]{0,1,2:T(8,128)S(1)}, f32[75,32,4]{0,1,2:T(8,128)S(1)}, u32[]{:S(2)}, u32[]{:S(2)}) collective-permute-start(f32[75,32,4]{0,1,2:T(8,128)S(1)} %get-tuple-element.24), channel_id=1, source_target_pairs={{4,0},{8,4},{12,8},{16,12},{20,16},{24,20},{28,24},{0,28},{5,1},{9... | collective-permute-start | bytes 115208 | tf_op jit(solution)/shard_map/ppermute | solution.py:17
  26.3 1.4 collective-permute-done
  27.9 3.5 collective-permute-start.2
  31.4 0.7 copy.78
  32.2 1.2 pad_maximum_fusion.7
  33.4 1.8 collective-permute-start.6
  35.2 0.9 copy.84
  36.2 0.6 broadcast_clamp_fusion
  36.8 1.0 copy.79
  37.8 3.0 collective-permute-done.3
  40.9 1.0 copy.80
  41.9 2.3 pad_maximum_fusion.1
  44.2 10.0 %collective-permute-done.6 = f32[3,75,4,136]{1,3,2,0:T(8,128)} collective-permute-done((f32[3,75,4,136]{1,3,2,0:T(8,128)S(1)}, f32[3,75,4,136]{1,3,2,0:T(8,128)}, u32[]{:S(2)}, u32[]{:S(2)}) %collective-permute-start.6) | collective-permute-done | bytes 489632 | tf_op jit(solution)/shard_map/ppermute | solution.py:16
  54.2 1.4 copy.85
  55.6 0.8 collective-permute-done.7
  56.3 1.4 copy.86
  57.7 4.9 %pad_maximum_fusion = f32[3,75,40,136]{1,2,3,0:T(8,128)S(1)} fusion(f32[3,75,4,136]{1,2,3,0:T(4,128)S(1)} %copy.86, f32[3,75,32,4]{1,2,3,0:T(8,128)} %collective-permute-done.5, f32[1,75,32,128]{1,2,3,0:T(8,128)S(1)} %bitcast.45, f32[1,75,32,128]{1,2,3,0:T(8,128)S(1)} %bitcast.42, f32[1,75,32,128]{1,2,3,0:T(8,128)S(1)} %copy-done.6, ...), kind=kLoop, calls=%fused_computation.6 | loop fusion | flops 7344000 | bytes 9792000 | tf_op jit(solution)/shard_map/concatenate | solution.py:18
  64.0 3.1 fusion.12
  67.2 3.1 fusion.28
  70.3 3.1 fusion.44
  73.4 2.2 fusion.62
  75.6 1.2 copy.87
  76.9 54.8 %gather_fusion = f32[16384,75]{1,0:T(8,128)} fusion(f32[75,4096]{0,1:T(8,128)S(1)} %bitcast.39, s32[16384]{0:T(1024)S(1)} %copy-done.19), kind=kCustom, calls=%fused_computation | custom fusion | bytes 9895936 | tf_op jit(solution)/shard_map/jit(_take)/gather | solution.py:76
  131.6 6.9 %multiply_reduce_fusion = f32[75,4096]{0,1:T(8,128)S(1)} fusion(f32[75,4,4096]{0,2,1:T(8,128)} %bitcast.46, f32[4,4096]{1,0:T(4,128)S(1)} %copy-done.18, pred[4,4096]{1,0:T(4,128)(4,1)S(1)} %compare_and_fusion), kind=kLoop, calls=%fused_computation.5 | loop fusion | flops 3379200 | bytes 6225920 | tf_op jit(solution)/shard_map/reduce_sum | solution.py:77
  138.6 1.7 copy.89
  140.3 6.5 %all-to-all-start = ((f32[75,32,128]{2,0,1:T(8,128)}), f32[75,32,128]{2,0,1:T(8,128)S(1)}, u32[]{:S(2)}, u32[]{:S(2)}) async-start(f32[75,32,128]{2,0,1:T(8,128)} %copy.89), calls=%async_computation | async-start | bytes 2621440 | tf_op jit(solution)/shard_map/all_to_all | solution.py:81
  146.8 1.8 copy.91
  148.7 2.8 copy.92
  151.6 26.1 %all-to-all-done = f32[75,32,128]{2,0,1:T(8,128)S(1)} async-done(((f32[75,32,128]{2,0,1:T(8,128)}), f32[75,32,128]{2,0,1:T(8,128)S(1)}, u32[]{:S(2)}, u32[]{:S(2)}) %all-to-all-start) | async-done | bytes 1228832 | tf_op jit(solution)/shard_map/all_to_all | solution.py:81
  177.6 1.8 copy.90
  179.5 3.2 fusion.70
  182.7 1.7 copy.93
  184.4 4.6 %all-to-all-start.1 = ((f32[75,32,128]{2,0,1:T(8,128)}), f32[75,32,128]{2,0,1:T(8,128)S(1)}, u32[]{:S(2)}, u32[]{:S(2)}) async-start(f32[75,32,128]{2,0,1:T(8,128)} %copy.93), calls=%async_computation.1 | async-start | bytes 2621440 | tf_op jit(solution)/shard_map/all_to_all | solution.py:84
  189.0 30.8 %all-to-all-done.1 = f32[75,32,128]{2,0,1:T(8,128)S(1)} async-done(((f32[75,32,128]{2,0,1:T(8,128)}), f32[75,32,128]{2,0,1:T(8,128)S(1)}, u32[]{:S(2)}, u32[]{:S(2)}) %all-to-all-start.1) | async-done | bytes 1228832 | tf_op jit(solution)/shard_map/all_to_all | solution.py:84
  219.8 1.8 copy.108
  221.6 6.0 %bitcast_multiply_fusion = f32[75,16384]{0,1:T(8,128)} fusion(f32[75,4096]{0,1:T(8,128)} %bitcast.51, f32[16384]{0:T(1024)S(1)} %bitcast.53), kind=kLoop, calls=%fused_computation.4 | loop fusion | flops 1228800 | bytes 6209536 | tf_op jit(solution)/shard_map/mul | solution.py:85
  227.6 81.0 %scatter_custom_fusion = f32[75,4096]{0,1:T(8,128)} fusion(s32[16384]{0:T(1024)} %bitcast.56, f32[75,16384]{0,1:T(8,128)} %bitcast_multiply_fusion, f32[]{:T(128)} %constant.9.clone.1), kind=kCustom, calls=%fused_computation.2 | custom fusion | flops 1228800 | bytes 9617920 | tf_op jit(solution)/shard_map/scatter-add | solution.py:86
  308.7 1.0 fusion.74
  309.7 1.4 collective-permute-start.8
  311.1 2.8 collective-permute-start.9
  313.9 1.7 collective-permute-done.8
  315.6 2.8 constant_dynamic-update-slice_fusion.1
  318.4 1.4 copy-done.13
  319.9 3.5 %collective-permute-start.10 = (f32[75,4,136]{0,2,1:T(8,128)S(1)}, f32[75,4,136]{0,2,1:T(8,128)S(1)}, u32[]{:S(2)}, u32[]{:S(2)}) collective-permute-start(f32[75,4,136]{0,2,1:T(8,128)S(1)} %copy.99), channel_id=1, source_target_pairs={{0,1},{1,2},{2,3},{3,0},{4,5},{5,6},{6,7},{7,4},{8,9},{9,10},{10,1... | collective-permute-start | bytes 489608 | tf_op jit(solution)/shard_map/ppermute | solution.py:16
  323.8 1.7 copy.105
  325.5 3.2 collective-permute-done.10
  328.8 1.8 collective-permute-done.11
  330.7 2.3 pad_maximum_fusion.2
  333.2 0.8 copy-done.3
  334.0 2.9 fusion.4
  336.9 3.0 fusion.20
  340.0 3.0 fusion.36
  343.0 2.6 fusion.54
  345.6 2.1 copy.104
  (74 shorter events, 2.8 us)
Async XLA Ops:
  3.0 16.6 %copy-start.4 = (s32[75,32,128]{0,1,2:T(8,128)}, s32[75,32,128]{0,1,2:T(8,128)S(1)}, u32[]{:S(2)}) copy-start(s32[75,32,128]{0,1,2:T(8,128)S(1)} %copy.75) | copy-start | bytes 3686404
  3.0 2.2 copy-start.15
  10.5 7.0 %copy-start.16 = (f32[75,32,128]{2,1,0:T(8,128)S(1)}, f32[75,32,128]{2,1,0:T(8,128)}, u32[]{:S(2)}) copy-start(f32[75,32,128]{2,1,0:T(8,128)} %param.9) | copy-start | bytes 3686404
  12.4 19.7 %collective-permute-start.4 = (f32[3,75,32,4]{1,2,3,0:T(8,128)}, f32[3,75,32,4]{1,2,3,0:T(8,128)S(1)}, u32[]{:S(2)}, u32[]{:S(2)}) collective-permute-start(f32[3,75,32,4]{1,2,3,0:T(8,128)} %get-tuple-element.15), channel_id=1, source_target_pairs={{0,4},{4,8},{8,12},{12,16},{16,20},{20,24},{24,28},{28,0},{1,5},{5... | collective-permute-start | bytes 345608 | tf_op jit(solution)/shard_map/ppermute | solution.py:16
  14.4 17.7 %collective-permute-start.5 = (f32[3,75,32,4]{1,2,3,0:T(8,128)}, f32[3,75,32,4]{1,2,3,0:T(8,128)}, u32[]{:S(2)}, u32[]{:S(2)}) collective-permute-start(f32[3,75,32,4]{1,2,3,0:T(8,128)} %get-tuple-element.16), channel_id=1, source_target_pairs={{4,0},{8,4},{12,8},{16,12},{20,16},{24,20},{28,24},{0,28},{5,1},{9... | collective-permute-start | bytes 345608 | tf_op jit(solution)/shard_map/ppermute | solution.py:17
  19.6 6.5 %copy-start.20 = (s32[4,4096]{1,0:T(4,128)S(1)}, s32[4,4096]{1,0:T(4,128)}, u32[]{:S(2)}) copy-start(s32[4,4096]{1,0:T(4,128)} %param.13) | copy-start | bytes 196612
  19.6 12.5 %copy-start.9 = (f32[75,32,128]{0,1,2:T(8,128)S(1)}, f32[75,32,128]{0,1,2:T(8,128)}, u32[]{:S(2)}) copy-start(f32[75,32,128]{0,1,2:T(8,128)} %copy.82) | copy-start | bytes 3686404
  21.8 5.9 %copy-start.11 = (f32[75,32,128]{0,1,2:T(8,128)}, f32[75,32,128]{0,1,2:T(8,128)S(1)}, u32[]{:S(2)}) copy-start(f32[75,32,128]{0,1,2:T(8,128)S(1)} %convert_multiply_fusion) | copy-start | bytes 3686404
  21.8 10.3 %copy-start.6 = (f32[1,75,32,128]{1,2,3,0:T(8,128)S(1)}, f32[1,75,32,128]{1,2,3,0:T(8,128)}, u32[]{:S(2)}) copy-start(f32[1,75,32,128]{1,2,3,0:T(8,128)} %convert_bitcast_fusion) | copy-start | bytes 3686404
  21.8 10.3 %copy-start.7 = (f32[75,32,128]{0,1,2:T(8,128)S(1)}, f32[75,32,128]{0,1,2:T(8,128)}, u32[]{:S(2)}) copy-start(f32[75,32,128]{0,1,2:T(8,128)} %copy.81) | copy-start | bytes 3686404
  21.9 5.9 %collective-permute-start = (f32[75,32,4]{0,1,2:T(8,128)S(1)}, f32[75,32,4]{0,1,2:T(8,128)S(1)}, u32[]{:S(2)}, u32[]{:S(2)}) collective-permute-start(f32[75,32,4]{0,1,2:T(8,128)S(1)} %get-tuple-element.23), channel_id=1, source_target_pairs={{0,4},{4,8},{8,12},{12,16},{16,20},{20,24},{24,28},{28,0},{1,5},{5... | collective-permute-start | bytes 115208 | tf_op jit(solution)/shard_map/ppermute | solution.py:16
  21.9 5.8 %collective-permute-start.1 = (f32[75,32,4]{0,1,2:T(8,128)S(1)}, f32[75,32,4]{0,1,2:T(8,128)S(1)}, u32[]{:S(2)}, u32[]{:S(2)}) collective-permute-start(f32[75,32,4]{0,1,2:T(8,128)S(1)} %get-tuple-element.24), channel_id=1, source_target_pairs={{4,0},{8,4},{12,8},{16,12},{20,16},{24,20},{28,24},{0,28},{5,1},{9... | collective-permute-start | bytes 115208 | tf_op jit(solution)/shard_map/ppermute | solution.py:17
  26.2 9.9 %copy-start.21 = (s32[16384,1]{0,1:T(1,128)}, s32[16384,1]{0,1:T(1,128)S(1)}, u32[]{:S(2)}) copy-start(s32[16384,1]{0,1:T(1,128)S(1)} %compare_select_fusion) | copy-start | bytes 196612
  27.7 5.6 %copy-start.17 = (f32[75,32,4]{0,1,2:T(8,128)}, f32[75,32,4]{0,1,2:T(8,128)S(1)}, u32[]{:S(2)}) copy-start(f32[75,32,4]{0,1,2:T(8,128)S(1)} %collective-permute-done.1) | copy-start | bytes 115204
  27.9 8.9 %collective-permute-start.2 = (f32[75,4,136]{0,2,1:T(8,128)S(1)}, f32[75,4,136]{0,2,1:T(8,128)}, u32[]{:S(2)}, u32[]{:S(2)}) collective-permute-start(f32[75,4,136]{0,2,1:T(8,128)S(1)} %copy.77), channel_id=1, source_target_pairs={{0,1},{1,2},{2,3},{3,0},{4,5},{5,6},{6,7},{7,4},{8,9},{9,10},{10,1... | collective-permute-start | bytes 489608 | tf_op jit(solution)/shard_map/ppermute | solution.py:16
  32.1 8.8 %collective-permute-start.3 = (f32[75,4,136]{0,2,1:T(8,128)}, f32[75,4,136]{0,2,1:T(8,128)}, u32[]{:S(2)}, u32[]{:S(2)}) collective-permute-start(f32[75,4,136]{0,2,1:T(8,128)} %copy.78), channel_id=1, source_target_pairs={{1,0},{2,1},{3,2},{0,3},{5,4},{6,5},{7,6},{4,7},{9,8},{10,9},{11,1... | collective-permute-start | bytes 489608 | tf_op jit(solution)/shard_map/ppermute | solution.py:17
  33.4 20.8 %collective-permute-start.6 = (f32[3,75,4,136]{1,3,2,0:T(8,128)S(1)}, f32[3,75,4,136]{1,3,2,0:T(8,128)}, u32[]{:S(2)}, u32[]{:S(2)}) collective-permute-start(f32[3,75,4,136]{1,3,2,0:T(8,128)S(1)} %copy.83), channel_id=1, source_target_pairs={{0,1},{1,2},{2,3},{3,0},{4,5},{5,6},{6,7},{7,4},{8,9},{9,10},{10,1... | collective-permute-start | bytes 1468808 | tf_op jit(solution)/shard_map/ppermute | solution.py:16
  36.2 20.2 %collective-permute-start.7 = (f32[3,75,4,136]{1,3,2,0:T(8,128)}, f32[3,75,4,136]{1,3,2,0:T(8,128)}, u32[]{:S(2)}, u32[]{:S(2)}) collective-permute-start(f32[3,75,4,136]{1,3,2,0:T(8,128)} %copy.84), channel_id=1, source_target_pairs={{1,0},{2,1},{3,2},{0,3},{5,4},{6,5},{7,6},{4,7},{9,8},{10,9},{11,1... | collective-permute-start | bytes 1468808 | tf_op jit(solution)/shard_map/ppermute | solution.py:17
  41.9 15.8 %copy-start.10 = (f32[75,32,128]{0,1,2:T(8,128)S(1)}, f32[75,32,128]{0,1,2:T(8,128)}, u32[]{:S(2)}) copy-start(f32[75,32,128]{0,1,2:T(8,128)} %copy.82) | copy-start | bytes 3686404
  44.2 13.5 %copy-start.8 = (f32[75,32,128]{0,1,2:T(8,128)S(1)}, f32[75,32,128]{0,1,2:T(8,128)}, u32[]{:S(2)}) copy-start(f32[75,32,128]{0,1,2:T(8,128)} %copy.81) | copy-start | bytes 3686404
  63.5 9.9 %copy-start = (f32[75,40,135]{0,1,2:T(8,128)}, f32[75,40,135]{0,1,2:T(8,128)S(1)}, u32[]{:S(2)}) copy-start(f32[75,40,135]{0,1,2:T(8,128)S(1)} %slice_multiply_fusion.2) | copy-start | bytes 4860004
  64.0 9.3 %copy-start.2 = (f32[75,39,136]{0,1,2:T(8,128)}, f32[75,39,136]{0,1,2:T(8,128)S(1)}, u32[]{:S(2)}) copy-start(f32[75,39,136]{0,1,2:T(8,128)S(1)} %fusion.2) | copy-start | bytes 4773604
  75.6 1.2 copy-start.19
  76.9 54.8 %copy-start.18 = (f32[4,4096]{1,0:T(4,128)S(1)}, f32[4,4096]{1,0:T(4,128)}, u32[]{:S(2)}) copy-start(f32[4,4096]{1,0:T(4,128)} %param.14) | copy-start | bytes 196612
  138.6 8.2 %copy-start.14 = (f32[75,4096]{1,0:T(8,128)S(1)}, f32[75,4096]{1,0:T(8,128)}, u32[]{:S(2)}) copy-start(f32[75,4096]{1,0:T(8,128)} %param.15) | copy-start | bytes 3686404
  140.3 37.3 %all-to-all-start = ((f32[75,32,128]{2,0,1:T(8,128)}), f32[75,32,128]{2,0,1:T(8,128)S(1)}, u32[]{:S(2)}, u32[]{:S(2)}) async-start(f32[75,32,128]{2,0,1:T(8,128)} %copy.89), calls=%async_computation | async-start | bytes 2621440 | tf_op jit(solution)/shard_map/all_to_all | solution.py:81
  146.8 4.7 %copy-start.22 = (s32[1,32]{1,0:T(1,128)S(1)}, s32[1,32]{1,0:T(1,128)}, u32[]{:S(2)}) copy-start(s32[1,32]{1,0:T(1,128)} %param.17) | copy-start | bytes 388
  184.4 35.4 %all-to-all-start.1 = ((f32[75,32,128]{2,0,1:T(8,128)}), f32[75,32,128]{2,0,1:T(8,128)S(1)}, u32[]{:S(2)}, u32[]{:S(2)}) async-start(f32[75,32,128]{2,0,1:T(8,128)} %copy.93), calls=%async_computation.1 | async-start | bytes 2621440 | tf_op jit(solution)/shard_map/all_to_all | solution.py:84
  309.7 5.9 %collective-permute-start.8 = (f32[75,32,4]{0,1,2:T(8,128)S(1)}, f32[75,32,4]{0,1,2:T(8,128)S(1)}, u32[]{:S(2)}, u32[]{:S(2)}) collective-permute-start(f32[75,32,4]{0,1,2:T(8,128)S(1)} %copy.113), channel_id=1, source_target_pairs={{0,4},{4,8},{8,12},{12,16},{16,20},{20,24},{24,28},{28,0},{1,5},{5... | collective-permute-start | bytes 115208 | tf_op jit(solution)/shard_map/ppermute | solution.py:16
  311.1 7.3 %collective-permute-start.9 = (f32[75,32,4]{0,1,2:T(8,128)S(1)}, f32[75,32,4]{0,1,2:T(8,128)S(1)}, u32[]{:S(2)}, u32[]{:S(2)}) collective-permute-start(f32[75,32,4]{0,1,2:T(8,128)S(1)} %copy.114), channel_id=1, source_target_pairs={{4,0},{8,4},{12,8},{16,12},{20,16},{24,20},{28,24},{0,28},{5,1},{9... | collective-permute-start | bytes 115208 | tf_op jit(solution)/shard_map/ppermute | solution.py:17
  318.4 1.4 copy-start.13
  319.9 8.8 %collective-permute-start.10 = (f32[75,4,136]{0,2,1:T(8,128)S(1)}, f32[75,4,136]{0,2,1:T(8,128)S(1)}, u32[]{:S(2)}, u32[]{:S(2)}) collective-permute-start(f32[75,4,136]{0,2,1:T(8,128)S(1)} %copy.99), channel_id=1, source_target_pairs={{0,1},{1,2},{2,3},{3,0},{4,5},{5,6},{6,7},{7,4},{8,9},{9,10},{10,1... | collective-permute-start | bytes 489608 | tf_op jit(solution)/shard_map/ppermute | solution.py:16
  323.5 7.2 %collective-permute-start.11 = (f32[75,4,136]{0,2,1:T(8,128)S(1)}, f32[75,4,136]{0,2,1:T(8,128)S(1)}, u32[]{:S(2)}, u32[]{:S(2)}) collective-permute-start(f32[75,4,136]{0,2,1:T(8,128)S(1)} %copy.100), channel_id=1, source_target_pairs={{1,0},{2,1},{3,2},{0,3},{5,4},{6,5},{7,6},{4,7},{9,8},{10,9},{11,1... | collective-permute-start | bytes 489608 | tf_op jit(solution)/shard_map/ppermute | solution.py:17
  330.7 2.5 copy-start.1
  330.7 3.3 copy-start.3
  340.0 3.0 copy-start.5
  340.0 3.0 copy-start.12
where the time goes:
time: 348 us
  other arithmetic  138 us (40%)
  local copies, waits for them, and re-layouts  95.6 us (27%)
  waiting for transfers between devices  78.9 us (23%)
  starting transfers between devices  33.7 us (10%)
    scatter-add x1, other arithmetic, body(): jnp.zeros((levels, tile_rows * tile_cols), jnp.float32).at[:, cell_list]  81 us
    gather x1, local copies, waits for them, and re-layouts, body(): picked = jnp.take(flat, cell_list, axis=1).reshape(levels, corners, -1)  54.8 us
    all_to_all x1, waiting for transfers between devices, body(): lax.all_to_all(departures, ('gx', 'gy'), split_axis=1, concat_axis=1, til...  30.8 us
    all_to_all x1, waiting for transfers between devices, body(): lax.all_to_all(equivalent, ('gx', 'gy'), split_axis=1, concat_axis=1, til...  26.1 us
    unnamed x60, local copies, waits for them, and re-layouts  24.1 us
    sub x7, other arithmetic, sweep(): centre + east[:, 1:-1, 1:-1] * (padded[:, 1:-1, 2:] - centre)  20.4 us
    ppermute x6, waiting for transfers between devices, with_halo(): before = lax.ppermute(last, axis, up)  16.4 us
    ppermute x6, starting transfers between devices, with_halo(): before = lax.ppermute(last, axis, up)  12.2 us
  transfers between devices with their start and end apart: 14, of which 9 were waited for; matrix products, arithmetic and copies ran while one was open for 7% of the time, Pallas kernels for 0%

commit v1 on v0

--- a/solution.py
+++ b/solution.py
@@ -81,7 +81,15 @@
     received = lax.all_to_all(equivalent, ("gx", "gy"), split_axis=1, concat_axis=1, tiled=True)
     live = (slot_counts[0][:, None] > jnp.arange(capacity)[None, :]).reshape(slots)
     departures = jnp.where(live[None, :], obs_precision * (received - obs_value), jnp.float32(0.0))
-    returned = lax.all_to_all(departures, ("gx", "gy"), split_axis=1, concat_axis=1, tiled=True)
+    returned = jnp.concatenate(
+        lax.all_to_all(
+            jnp.stack(jnp.split(departures, lax.axis_size(("gx", "gy")), axis=1)),
+            ("gx", "gy"),
+            0,
+            0,
+        ),
+        axis=1,
+    )
     spread = (corner_weights[None, :, :] * returned[:, None, :]).reshape(levels, -1)
     adjoint = jnp.zeros((levels, tile_rows * tile_cols), jnp.float32).at[:, cell_list].add(spread)
     gradient = masked * (control + diffuse(adjoint.reshape(levels, tile_rows, tile_cols)))

time: 348 us -> 370 us (1.063)
  local copies, waits for them, and re-layouts: 95.6 us -> 117 us
    unnamed x60 -> x91, local copies, waits for them, and re-layouts: 24.1 us -> 43.6 us
  transfers between devices with their start and end apart: 14 -> 14, of which waited for: 9 -> 9; matrix products, arithmetic and copies ran while one was open for 7% -> 6% of each run, Pallas kernels for 0% -> 0%
where the time goes in v1:
time: 370 us; the launch traced here: 369 us
  other arithmetic  138 us (37%)
  local copies, waits for them, and re-layouts  117 us (32%)
  waiting for transfers between devices  78.9 us (21%)
  starting transfers between devices  33.7 us (9%)
    scatter-add x1, other arithmetic, body(): jnp.zeros((levels, tile_rows * tile_cols), jnp.float32).at[:, cell_list]  81 us
    gather x1, local copies, waits for them, and re-layouts, body(): picked = jnp.take(flat, cell_list, axis=1).reshape(levels, corners, -1)  54.8 us
    unnamed x91, local copies, waits for them, and re-layouts  43.6 us
    all_to_all x1, waiting for transfers between devices, body(): lax.all_to_all(jnp.stack(jnp.split(departures, lax.axis_size(('gx', 'gy')...  30.8 us
    all_to_all x1, waiting for transfers between devices, body(): lax.all_to_all(equivalent, ('gx', 'gy'), split_axis=1, concat_axis=1, til...  26.1 us
    sub x7, other arithmetic, sweep(): centre + east[:, 1:-1, 1:-1] * (padded[:, 1:-1, 2:] - centre)  20.4 us
    ppermute x6, waiting for transfers between devices, with_halo(): before = lax.ppermute(last, axis, up)  16.4 us
    ppermute x6, starting transfers between devices, with_halo(): before = lax.ppermute(last, axis, up)  12.2 us
  transfers between devices with their start and end apart: 14, of which 9 were waited for; matrix products, arithmetic and copies ran while one was open for 6% of the time, Pallas kernels for 0%

profile of v1, /device:TPU:1, one launch (start us, length us, event | category | flops | bytes accessed | tf_op | source)
XLA Modules:
  0.0 368.9 jit_solution(10406987945311123805)
XLA Ops:
  0.6 2.4 copy.75
  3.0 1.6 convert_bitcast_fusion
  5.2 2.2 copy.81
  7.4 3.1 copy.82
  10.5 1.9 pad_maximum_fusion.13
  12.4 2.0 collective-permute-start.4
  14.4 3.0 collective-permute-start.5
  17.4 2.1 copy.103
  19.6 2.2 convert_multiply_fusion
  21.9 4.1 %collective-permute-start.1 = (f32[75,32,4]{0,1,2:T(8,128)S(1)}, f32[75,32,4]{0,1,2:T(8,128)S(1)}, u32[]{:S(2)}, u32[]{:S(2)}) collective-permute-start(f32[75,32,4]{0,1,2:T(8,128)S(1)} %get-tuple-element.24), channel_id=1, source_target_pairs={{4,0},{8,4},{12,8},{16,12},{20,16},{24,20},{28,24},{0,28},{5,1},{9... | collective-permute-start | bytes 115208 | tf_op jit(solution)/shard_map/ppermute | solution.py:17
  26.3 1.4 collective-permute-done
  27.9 3.5 collective-permute-start.2
  31.4 0.7 copy.78
  32.2 1.2 pad_maximum_fusion.7
  33.4 1.8 collective-permute-start.6
  35.2 0.9 copy.84
  36.8 1.0 copy.79
  37.8 3.0 collective-permute-done.3
  40.9 1.0 copy.80
  41.9 2.3 pad_maximum_fusion.1
  44.2 10.0 %collective-permute-done.6 = f32[3,75,4,136]{1,3,2,0:T(8,128)} collective-permute-done((f32[3,75,4,136]{1,3,2,0:T(8,128)S(1)}, f32[3,75,4,136]{1,3,2,0:T(8,128)}, u32[]{:S(2)}, u32[]{:S(2)}) %collective-permute-start.6) | collective-permute-done | bytes 489632 | tf_op jit(solution)/shard_map/ppermute | solution.py:16
  54.2 1.4 copy.85
  55.6 0.8 collective-permute-done.7
  56.3 1.4 copy.86
  57.7 4.9 %pad_maximum_fusion = f32[3,75,40,136]{1,2,3,0:T(8,128)S(1)} fusion(f32[3,75,4,136]{1,2,3,0:T(4,128)S(1)} %copy.86, f32[3,75,32,4]{1,2,3,0:T(8,128)} %collective-permute-done.5, f32[1,75,32,128]{1,2,3,0:T(8,128)S(1)} %bitcast.173, f32[1,75,32,128]{1,2,3,0:T(8,128)S(1)} %bitcast.170, f32[1,75,32,128]{1,2,3,0:T(8,128)S(1)} %copy-done.6, ...), kind=kLoop, calls=%fused_computation.6 | loop fusion | flops 7344000 | bytes 9792000 | tf_op jit(solution)/shard_map/concatenate | solution.py:18
  64.0 3.1 fusion.12
  67.2 3.1 fusion.28
  70.3 3.1 fusion.44
  73.4 2.2 fusion.62
  75.6 1.2 copy.87
  76.9 54.8 %gather_fusion = f32[16384,75]{1,0:T(8,128)} fusion(f32[75,4096]{0,1:T(8,128)S(1)} %bitcast.167, s32[16384]{0:T(1024)S(1)} %copy-done.19), kind=kCustom, calls=%fused_computation | custom fusion | bytes 9895936 | tf_op jit(solution)/shard_map/jit(_take)/gather | solution.py:76
  131.6 6.9 %multiply_reduce_fusion = f32[75,4096]{0,1:T(8,128)S(1)} fusion(f32[75,4,4096]{0,2,1:T(8,128)} %bitcast.174, f32[4,4096]{1,0:T(4,128)S(1)} %copy-done.18, pred[4,4096]{1,0:T(4,128)(4,1)S(1)} %compare_and_fusion), kind=kLoop, calls=%fused_computation.5 | loop fusion | flops 3379200 | bytes 6225920 | tf_op jit(solution)/shard_map/reduce_sum | solution.py:77
  138.6 1.7 copy.89
  140.3 6.5 %all-to-all-start = ((f32[75,32,128]{2,0,1:T(8,128)}), f32[75,32,128]{2,0,1:T(8,128)S(1)}, u32[]{:S(2)}, u32[]{:S(2)}) async-start(f32[75,32,128]{2,0,1:T(8,128)} %copy.89), calls=%async_computation | async-start | bytes 2621440 | tf_op jit(solution)/shard_map/all_to_all | solution.py:81
  146.8 1.8 copy.91
  148.7 2.8 copy.92
  151.6 26.1 %all-to-all-done = f32[75,32,128]{2,0,1:T(8,128)S(1)} async-done(((f32[75,32,128]{2,0,1:T(8,128)}), f32[75,32,128]{2,0,1:T(8,128)S(1)}, u32[]{:S(2)}, u32[]{:S(2)}) %all-to-all-start) | async-done | bytes 1228832 | tf_op jit(solution)/shard_map/all_to_all | solution.py:81
  177.6 1.8 copy.90
  179.5 3.2 fusion.70
  185.8 0.6 constant_dynamic-update-slice_fusion.26
  196.5 0.6 constant_dynamic-update-slice_fusion.9
  202.8 2.8 copy.93
  205.6 4.6 %all-to-all-start.1 = ((f32[32,75,128]{2,1,0:T(8,128)}), f32[32,75,128]{2,1,0:T(8,128)S(1)}, u32[]{:S(2)}, u32[]{:S(2)}) async-start(f32[32,75,128]{2,1,0:T(8,128)} %copy.93), calls=%async_computation.1 | async-start | bytes 2621440 | tf_op jit(solution)/shard_map/all_to_all | solution.py:85
  210.2 30.8 %all-to-all-done.1 = f32[32,75,128]{2,1,0:T(8,128)S(1)} async-done(((f32[32,75,128]{2,1,0:T(8,128)}), f32[32,75,128]{2,1,0:T(8,128)S(1)}, u32[]{:S(2)}, u32[]{:S(2)}) %all-to-all-start.1) | async-done | bytes 1228832 | tf_op jit(solution)/shard_map/all_to_all | solution.py:85
  241.0 1.8 copy.108
  242.8 6.0 %bitcast_multiply_fusion = f32[75,16384]{0,1:T(8,128)} fusion(f32[75,4096]{0,1:T(8,128)} %bitcast.178, f32[16384]{0:T(1024)S(1)} %bitcast.181), kind=kLoop, calls=%fused_computation.4 | loop fusion | flops 1228800 | bytes 6209536 | tf_op jit(solution)/shard_map/mul | solution.py:93
  248.9 81.0 %scatter_custom_fusion = f32[75,4096]{0,1:T(8,128)} fusion(s32[16384]{0:T(1024)} %bitcast.184, f32[75,16384]{0,1:T(8,128)} %bitcast_multiply_fusion, f32[]{:T(128)} %constant.9.clone.1), kind=kCustom, calls=%fused_computation.2 | custom fusion | flops 1228800 | bytes 9617920 | tf_op jit(solution)/shard_map/scatter-add | solution.py:94
  329.9 1.0 fusion.74
  330.9 1.4 collective-permute-start.8
  332.3 2.8 collective-permute-start.9
  335.1 1.7 collective-permute-done.8
  336.8 2.8 constant_dynamic-update-slice_fusion.33
  339.6 1.4 copy-done.13
  341.1 3.5 collective-permute-start.10
  345.0 1.7 copy.105
  346.7 3.2 collective-permute-done.10
  350.0 1.8 collective-permute-done.11
  351.9 2.3 pad_maximum_fusion.2
  354.4 0.8 copy-done.3
  355.2 2.9 fusion.4
  358.1 3.0 fusion.20
  361.2 3.0 fusion.36
  364.2 2.6 fusion.54
  366.8 2.1 copy.104
  (106 shorter events, 22.8 us)
Async XLA Ops:
  3.0 16.6 %copy-start.4 = (s32[75,32,128]{0,1,2:T(8,128)}, s32[75,32,128]{0,1,2:T(8,128)S(1)}, u32[]{:S(2)}) copy-start(s32[75,32,128]{0,1,2:T(8,128)S(1)} %copy.75) | copy-start | bytes 3686404
  3.0 2.2 copy-start.15
  10.5 7.0 %copy-start.16 = (f32[75,32,128]{2,1,0:T(8,128)S(1)}, f32[75,32,128]{2,1,0:T(8,128)}, u32[]{:S(2)}) copy-start(f32[75,32,128]{2,1,0:T(8,128)} %param.9) | copy-start | bytes 3686404
  12.4 19.7 %collective-permute-start.4 = (f32[3,75,32,4]{1,2,3,0:T(8,128)}, f32[3,75,32,4]{1,2,3,0:T(8,128)S(1)}, u32[]{:S(2)}, u32[]{:S(2)}) collective-permute-start(f32[3,75,32,4]{1,2,3,0:T(8,128)} %get-tuple-element.15), channel_id=1, source_target_pairs={{0,4},{4,8},{8,12},{12,16},{16,20},{20,24},{24,28},{28,0},{1,5},{5... | collective-permute-start | bytes 345608 | tf_op jit(solution)/shard_map/ppermute | solution.py:16
  14.4 17.7 %collective-permute-start.5 = (f32[3,75,32,4]{1,2,3,0:T(8,128)}, f32[3,75,32,4]{1,2,3,0:T(8,128)}, u32[]{:S(2)}, u32[]{:S(2)}) collective-permute-start(f32[3,75,32,4]{1,2,3,0:T(8,128)} %get-tuple-element.16), channel_id=1, source_target_pairs={{4,0},{8,4},{12,8},{16,12},{20,16},{24,20},{28,24},{0,28},{5,1},{9... | collective-permute-start | bytes 345608 | tf_op jit(solution)/shard_map/ppermute | solution.py:17
  19.6 6.5 %copy-start.20 = (s32[4,4096]{1,0:T(4,128)S(1)}, s32[4,4096]{1,0:T(4,128)}, u32[]{:S(2)}) copy-start(s32[4,4096]{1,0:T(4,128)} %param.13) | copy-start | bytes 196612
  19.6 12.5 %copy-start.9 = (f32[75,32,128]{0,1,2:T(8,128)S(1)}, f32[75,32,128]{0,1,2:T(8,128)}, u32[]{:S(2)}) copy-start(f32[75,32,128]{0,1,2:T(8,128)} %copy.82) | copy-start | bytes 3686404
  21.8 10.3 %copy-start.11 = (f32[75,32,128]{0,1,2:T(8,128)}, f32[75,32,128]{0,1,2:T(8,128)S(1)}, u32[]{:S(2)}) copy-start(f32[75,32,128]{0,1,2:T(8,128)S(1)} %convert_multiply_fusion) | copy-start | bytes 3686404
  21.8 10.3 %copy-start.6 = (f32[1,75,32,128]{1,2,3,0:T(8,128)S(1)}, f32[1,75,32,128]{1,2,3,0:T(8,128)}, u32[]{:S(2)}) copy-start(f32[1,75,32,128]{1,2,3,0:T(8,128)} %convert_bitcast_fusion) | copy-start | bytes 3686404
  21.8 10.3 %copy-start.7 = (f32[75,32,128]{0,1,2:T(8,128)S(1)}, f32[75,32,128]{0,1,2:T(8,128)}, u32[]{:S(2)}) copy-start(f32[75,32,128]{0,1,2:T(8,128)} %copy.81) | copy-start | bytes 3686404
  21.9 5.9 %collective-permute-start = (f32[75,32,4]{0,1,2:T(8,128)S(1)}, f32[75,32,4]{0,1,2:T(8,128)S(1)}, u32[]{:S(2)}, u32[]{:S(2)}) collective-permute-start(f32[75,32,4]{0,1,2:T(8,128)S(1)} %get-tuple-element.23), channel_id=1, source_target_pairs={{0,4},{4,8},{8,12},{12,16},{16,20},{20,24},{24,28},{28,0},{1,5},{5... | collective-permute-start | bytes 115208 | tf_op jit(solution)/shard_map/ppermute | solution.py:16
  21.9 5.8 %collective-permute-start.1 = (f32[75,32,4]{0,1,2:T(8,128)S(1)}, f32[75,32,4]{0,1,2:T(8,128)S(1)}, u32[]{:S(2)}, u32[]{:S(2)}) collective-permute-start(f32[75,32,4]{0,1,2:T(8,128)S(1)} %get-tuple-element.24), channel_id=1, source_target_pairs={{4,0},{8,4},{12,8},{16,12},{20,16},{24,20},{28,24},{0,28},{5,1},{9... | collective-permute-start | bytes 115208 | tf_op jit(solution)/shard_map/ppermute | solution.py:17
  26.2 9.9 %copy-start.21 = (s32[16384,1]{0,1:T(1,128)}, s32[16384,1]{0,1:T(1,128)S(1)}, u32[]{:S(2)}) copy-start(s32[16384,1]{0,1:T(1,128)S(1)} %compare_select_fusion) | copy-start | bytes 196612
  27.7 5.6 %copy-start.17 = (f32[75,32,4]{0,1,2:T(8,128)}, f32[75,32,4]{0,1,2:T(8,128)S(1)}, u32[]{:S(2)}) copy-start(f32[75,32,4]{0,1,2:T(8,128)S(1)} %collective-permute-done.1) | copy-start | bytes 115204
  27.9 8.9 %collective-permute-start.2 = (f32[75,4,136]{0,2,1:T(8,128)S(1)}, f32[75,4,136]{0,2,1:T(8,128)}, u32[]{:S(2)}, u32[]{:S(2)}) collective-permute-start(f32[75,4,136]{0,2,1:T(8,128)S(1)} %copy.77), channel_id=1, source_target_pairs={{0,1},{1,2},{2,3},{3,0},{4,5},{5,6},{6,7},{7,4},{8,9},{9,10},{10,1... | collective-permute-start | bytes 489608 | tf_op jit(solution)/shard_map/ppermute | solution.py:16
  32.1 8.8 %collective-permute-start.3 = (f32[75,4,136]{0,2,1:T(8,128)}, f32[75,4,136]{0,2,1:T(8,128)}, u32[]{:S(2)}, u32[]{:S(2)}) collective-permute-start(f32[75,4,136]{0,2,1:T(8,128)} %copy.78), channel_id=1, source_target_pairs={{1,0},{2,1},{3,2},{0,3},{5,4},{6,5},{7,6},{4,7},{9,8},{10,9},{11,1... | collective-permute-start | bytes 489608 | tf_op jit(solution)/shard_map/ppermute | solution.py:17
  33.4 20.8 %collective-permute-start.6 = (f32[3,75,4,136]{1,3,2,0:T(8,128)S(1)}, f32[3,75,4,136]{1,3,2,0:T(8,128)}, u32[]{:S(2)}, u32[]{:S(2)}) collective-permute-start(f32[3,75,4,136]{1,3,2,0:T(8,128)S(1)} %copy.83), channel_id=1, source_target_pairs={{0,1},{1,2},{2,3},{3,0},{4,5},{5,6},{6,7},{7,4},{8,9},{9,10},{10,1... | collective-permute-start | bytes 1468808 | tf_op jit(solution)/shard_map/ppermute | solution.py:16
  36.2 20.2 %collective-permute-start.7 = (f32[3,75,4,136]{1,3,2,0:T(8,128)}, f32[3,75,4,136]{1,3,2,0:T(8,128)}, u32[]{:S(2)}, u32[]{:S(2)}) collective-permute-start(f32[3,75,4,136]{1,3,2,0:T(8,128)} %copy.84), channel_id=1, source_target_pairs={{1,0},{2,1},{3,2},{0,3},{5,4},{6,5},{7,6},{4,7},{9,8},{10,9},{11,1... | collective-permute-start | bytes 1468808 | tf_op jit(solution)/shard_map/ppermute | solution.py:17
  41.9 15.8 %copy-start.10 = (f32[75,32,128]{0,1,2:T(8,128)S(1)}, f32[75,32,128]{0,1,2:T(8,128)}, u32[]{:S(2)}) copy-start(f32[75,32,128]{0,1,2:T(8,128)} %copy.82) | copy-start | bytes 3686404
  44.2 13.6 %copy-start.8 = (f32[75,32,128]{0,1,2:T(8,128)S(1)}, f32[75,32,128]{0,1,2:T(8,128)}, u32[]{:S(2)}) copy-start(f32[75,32,128]{0,1,2:T(8,128)} %copy.81) | copy-start | bytes 3686404
  63.5 9.9 %copy-start = (f32[75,40,135]{0,1,2:T(8,128)}, f32[75,40,135]{0,1,2:T(8,128)S(1)}, u32[]{:S(2)}) copy-start(f32[75,40,135]{0,1,2:T(8,128)S(1)} %slice_multiply_fusion.2) | copy-start | bytes 4860004
  64.0 9.3 %copy-start.2 = (f32[75,39,136]{0,1,2:T(8,128)}, f32[75,39,136]{0,1,2:T(8,128)S(1)}, u32[]{:S(2)}) copy-start(f32[75,39,136]{0,1,2:T(8,128)S(1)} %fusion.2) | copy-start | bytes 4773604
  75.6 1.2 copy-start.19
  76.8 54.8 %copy-start.18 = (f32[4,4096]{1,0:T(4,128)S(1)}, f32[4,4096]{1,0:T(4,128)}, u32[]{:S(2)}) copy-start(f32[4,4096]{1,0:T(4,128)} %param.14) | copy-start | bytes 196612
  138.6 8.2 %copy-start.14 = (f32[75,4096]{1,0:T(8,128)S(1)}, f32[75,4096]{1,0:T(8,128)}, u32[]{:S(2)}) copy-start(f32[75,4096]{1,0:T(8,128)} %param.15) | copy-start | bytes 3686404
  140.3 37.3 %all-to-all-start = ((f32[75,32,128]{2,0,1:T(8,128)}), f32[75,32,128]{2,0,1:T(8,128)S(1)}, u32[]{:S(2)}, u32[]{:S(2)}) async-start(f32[75,32,128]{2,0,1:T(8,128)} %copy.89), calls=%async_computation | async-start | bytes 2621440 | tf_op jit(solution)/shard_map/all_to_all | solution.py:81
  148.7 2.8 copy-start.22
  205.6 35.4 %all-to-all-start.1 = ((f32[32,75,128]{2,1,0:T(8,128)}), f32[32,75,128]{2,1,0:T(8,128)S(1)}, u32[]{:S(2)}, u32[]{:S(2)}) async-start(f32[32,75,128]{2,1,0:T(8,128)} %copy.93), calls=%async_computation.1 | async-start | bytes 2621440 | tf_op jit(solution)/shard_map/all_to_all | solution.py:85
  330.9 5.9 %collective-permute-start.8 = (f32[75,32,4]{0,1,2:T(8,128)S(1)}, f32[75,32,4]{0,1,2:T(8,128)S(1)}, u32[]{:S(2)}, u32[]{:S(2)}) collective-permute-start(f32[75,32,4]{0,1,2:T(8,128)S(1)} %copy.113), channel_id=1, source_target_pairs={{0,4},{4,8},{8,12},{12,16},{16,20},{20,24},{24,28},{28,0},{1,5},{5... | collective-permute-start | bytes 115208 | tf_op jit(solution)/shard_map/ppermute | solution.py:16
  332.3 7.3 %collective-permute-start.9 = (f32[75,32,4]{0,1,2:T(8,128)S(1)}, f32[75,32,4]{0,1,2:T(8,128)S(1)}, u32[]{:S(2)}, u32[]{:S(2)}) collective-permute-start(f32[75,32,4]{0,1,2:T(8,128)S(1)} %copy.114), channel_id=1, source_target_pairs={{4,0},{8,4},{12,8},{16,12},{20,16},{24,20},{28,24},{0,28},{5,1},{9... | collective-permute-start | bytes 115208 | tf_op jit(solution)/shard_map/ppermute | solution.py:17
  339.6 1.4 copy-start.13
  341.1 8.8 %collective-permute-start.10 = (f32[75,4,136]{0,2,1:T(8,128)S(1)}, f32[75,4,136]{0,2,1:T(8,128)S(1)}, u32[]{:S(2)}, u32[]{:S(2)}) collective-permute-start(f32[75,4,136]{0,2,1:T(8,128)S(1)} %copy.99), channel_id=1, source_target_pairs={{0,1},{1,2},{2,3},{3,0},{4,5},{5,6},{6,7},{7,4},{8,9},{9,10},{10,1... | collective-permute-start | bytes 489608 | tf_op jit(solution)/shard_map/ppermute | solution.py:16
  344.7 7.2 %collective-permute-start.11 = (f32[75,4,136]{0,2,1:T(8,128)S(1)}, f32[75,4,136]{0,2,1:T(8,128)S(1)}, u32[]{:S(2)}, u32[]{:S(2)}) collective-permute-start(f32[75,4,136]{0,2,1:T(8,128)S(1)} %copy.100), channel_id=1, source_target_pairs={{1,0},{2,1},{3,2},{0,3},{5,4},{6,5},{7,6},{4,7},{9,8},{10,9},{11,1... | collective-permute-start | bytes 489608 | tf_op jit(solution)/shard_map/ppermute | solution.py:17
  351.9 2.5 copy-start.1
  351.9 3.3 copy-start.3
  361.2 3.0 copy-start.5
  361.2 3.0 copy-start.12
